TPU v7x, 32 devices: a whole 2x2x4 slice. The times are simulated.
32 devices in a mesh: group: 4 (over x, core), replica: 8 (over z, y).
Axes of the slice: x: 2, y: 2, z: 4, core: 2. Of those that a mesh axis runs over, the one named last changes fastest.
Arguments:
- tokens: bfloat16 [16, 1024, 384], P('replica', 'group'), may hold values from -6 to 6
- cotangent: bfloat16 [16, 1024, 384], P('replica', 'group'), may hold values from -6 to 6
- weight: float32 [1774592], P('group'), may hold values from -1.6329932 to 1.6329932
- momentum: float32 [1774592], P('group'), may hold values from -40 to 40
- average: float32 [1774592], P('group'), may hold values from -1.6329932 to 1.6329932
- rate: float32 [1], replicated, may hold values from 0.00015625 to 0.000625
- step: int32 [1], replicated, may hold values from 1 to 20
Outputs:
- output: bfloat16 [16, 1024, 384], P('replica', 'group')
- grad_tokens: bfloat16 [16, 1024, 384], P('replica', 'group')
- grad: float32 [1774592], P('group')
- momentum_new: float32 [1774592], P('group')
- average_new: float32 [1774592], P('group')
- weight_new: float32 [1774592], P('group')
- weight_copy: bfloat16 [1774592], P('group')
All inputs are finite; a program needn't handle non-finite values.
Results may differ from a plain program's by a relative error of at most 0.013.
The roundings to bfloat16 on the way count: a program that leaves them out, or rounds other values in their place, can miss the bound.
Values may be sent and summed in bfloat16 or wider, within the bound.
No kernel may reach another device: no remote copies, remote signals or barrier semaphores. Data moves between devices by JAX's collectives and lax.ppermute only.
A program may use at most 448 MiB of HBM per device.

v0:
```python
from functools import partial
import jax
import jax.numpy as jnp
from jax import lax
from jax.sharding import PartitionSpec as P

D = 384
H = 6
DH = 64
FF = 1536
EPSILON = 1e-06
MOMENT = 0.9
DECAY_MAX = 0.999
INV_ROOT_TWO = 0.7071067811865476
INV_ROOT_TAU = 0.3989422804014327


def split_params(flat_vec):
    layout = (
        (D * 3 * D, (D, 3 * D)),
        (D * D, (D, D)),
        (D * FF, (D, FF)),
        (FF * D, (FF, D)),
        (D, (D,)),
        (D, (D,)),
        (3 * D, (3 * D,)),
        (DH, (DH,)),
        (DH, (DH,)),
        (D, (D,)),
        (D, (D,)),
        (D, (D,)),
        (FF, (FF,)),
        (D, (D,)),
    )
    pieces = []
    offset = 0
    for seg_len, seg_shape in layout:
        pieces.append(flat_vec[offset : offset + seg_len].reshape(seg_shape))
        offset = offset + seg_len
    return tuple(pieces)


def norm_forward(values, scale, shift):
    center = values - jnp.mean(values, -1, keepdims=True)
    inv_std = lax.rsqrt(jnp.mean(center * center, -1, keepdims=True) + EPSILON)
    normed = center * inv_std
    return (normed * scale + shift, normed, inv_std)


def norm_backward(grad_out, normed, inv_std, scale):
    grad_norm = grad_out * scale
    inner = jnp.mean(grad_norm * normed, -1, keepdims=True)
    return inv_std * (grad_norm - jnp.mean(grad_norm, -1, keepdims=True) - normed * inner)


def gelu_slope(values):
    return (
        0.5 * (1.0 + lax.erf(values * INV_ROOT_TWO))
        + values * jnp.exp(-0.5 * values * values) * INV_ROOT_TAU
    )


def cross_dot(left, right):
    return lax.dot_general(
        left, right, (((0,), (0,)), ((), ())), preferred_element_type=jnp.float32
    )


def back_dot(left, right):
    return lax.dot_general(
        left, right, (((1,), (1,)), ((), ())), preferred_element_type=jnp.float32
    )


def head_scores(query_b, key_block_rows, row_mask_values, scale_factor):
    query_masked = query_b * row_mask_values
    scores = (
        jnp.einsum("xuc,xlc->xul", query_masked, key_block_rows, preferred_element_type=jnp.float32)
        * scale_factor
    )
    return (query_masked, scores)


def attend_block(operands, masks, scale_factor):
    query_b, key_block_rows, value_block_rows = operands

    def attend_one_head(total, row_mask_values):
        query_masked, scores = head_scores(query_b, key_block_rows, row_mask_values, scale_factor)
        row_peak = jnp.max(scores, -1, keepdims=True)
        raised = jnp.exp(scores - row_peak)
        row_total = jnp.sum(raised, -1, keepdims=True)
        attention_weights = (raised / row_total).astype(jnp.bfloat16)
        part_out = jnp.einsum(
            "cxu,cuw->cxw",
            attention_weights,
            value_block_rows * row_mask_values,
            preferred_element_type=jnp.float32,
        )
        return (total + part_out, (row_peak + jnp.log(row_total))[..., 0])

    start = jnp.zeros(query_b.shape, jnp.float32)
    return lax.scan(attend_one_head, start, masks)


def head_grads(
    query_b, key_block_rows, value_block_rows, grad_b, log_h, inner_h, row_mask_values, scale_factor
):
    query_masked, scores = head_scores(query_b, key_block_rows, row_mask_values, scale_factor)
    probs = jnp.exp(scores - log_h[..., None])
    gradient_masked = grad_b * row_mask_values
    grad_probs = jnp.einsum(
        "xuc,xlc->xul", gradient_masked, value_block_rows, preferred_element_type=jnp.float32
    )
    inner_h = jnp.sum(probs * grad_probs, -1)
    score_gradient = (probs * (grad_probs - inner_h[..., None])).astype(jnp.bfloat16)
    return (probs, score_gradient, inner_h, query_masked, gradient_masked)


def local_back(operands, masks, scale_factor):
    query_b, key_block_rows, value_block_rows, grad_b, log_b = operands

    def local_one_head(carry, head_in):
        row_mask_values, log_h = head_in
        probs, score_gradient, inner_h, query_masked, gradient_masked = head_grads(
            query_b,
            key_block_rows,
            value_block_rows,
            grad_b,
            log_h,
            None,
            row_mask_values,
            scale_factor,
        )
        grad_query = (
            jnp.einsum(
                "cxu,cuw->cxw",
                score_gradient,
                key_block_rows * row_mask_values,
                preferred_element_type=jnp.float32,
            )
            * scale_factor
        )
        grad_key = (
            jnp.einsum(
                "fji,fjp->fip", score_gradient, query_masked, preferred_element_type=jnp.float32
            )
            * scale_factor
        )
        grad_value = jnp.einsum(
            "fji,fjp->fip",
            probs.astype(jnp.bfloat16),
            gradient_masked,
            preferred_element_type=jnp.float32,
        )
        return ((carry[0] + grad_query, carry[1] + grad_key, carry[2] + grad_value), None)

    start = (
        jnp.zeros(query_b.shape, jnp.float32),
        jnp.zeros(key_block_rows.shape, jnp.float32),
        jnp.zeros(key_block_rows.shape, jnp.float32),
    )
    totals, unused = lax.scan(local_one_head, start, (masks, log_b))
    return totals


def per_device(tokens, cotangent, weight, momentum, average, rate, step):
    image_count, own_len, width = tokens.shape
    row_count = image_count * own_len
    scale_factor = DH ** (-0.5)
    pair_size = 2
    head_masks = (
        lax.broadcasted_iota(jnp.int32, (H, width), 1) // DH
        == lax.broadcasted_iota(jnp.int32, (H, width), 0)
    ).astype(jnp.bfloat16)

    def in_blocks(array):
        return array.reshape((image_count // pair_size, pair_size) + array.shape[1:])

    def unblock(array):
        return array.reshape((image_count,) + array.shape[2:])

    shard_low = weight.astype(jnp.bfloat16)
    gathered = lax.all_gather(shard_low, "group", axis=0, tiled=True)
    (
        w_qkv,
        w_out,
        w_fc1,
        w_fc2,
        g_one,
        b_one,
        b_qkv,
        g_query,
        g_key,
        b_out,
        g_two,
        b_two,
        b_fc1,
        b_fc2,
    ) = split_params(gathered)
    (
        gain_one,
        bias_one,
        bias_qkv,
        gain_query,
        gain_key,
        bias_out,
        gain_two,
        bias_two,
        bias_fc1,
        bias_fc2,
    ) = tuple(
        (
            member.astype(jnp.float32)
            for member in (g_one, b_one, b_qkv, g_query, g_key, b_out, g_two, b_two, b_fc1, b_fc2)
        )
    )
    resid_in = tokens.astype(jnp.float32).reshape(row_count, width)
    ln_one_out, normed_one, inv_one = norm_forward(resid_in, gain_one, bias_one)
    act_one = ln_one_out.astype(jnp.bfloat16)
    qkv_full = jnp.dot(act_one, w_qkv, preferred_element_type=jnp.float32) + bias_qkv
    head_shape = (row_count, H, DH)
    query_pre = qkv_full[:, :width].reshape(head_shape)
    key_pre = qkv_full[:, width : 2 * width].reshape(head_shape)
    value_pre = qkv_full[:, 2 * width :]
    query_out, query_normed, query_inv = norm_forward(query_pre, gain_query, 0.0)
    key_out, key_normed, key_inv = norm_forward(key_pre, gain_key, 0.0)
    image_shape = (image_count, own_len, width)
    query_low = query_out.astype(jnp.bfloat16).reshape(image_shape)
    key_low = key_out.astype(jnp.bfloat16).reshape(image_shape)
    value_low = value_pre.astype(jnp.bfloat16).reshape(image_shape)
    key_all, value_all = (
        lax.all_gather(key_low, "group", axis=1, tiled=True),
        lax.all_gather(value_low, "group", axis=1, tiled=True),
    )
    attn_out, log_sum = lax.map(
        partial(attend_block, masks=head_masks, scale_factor=scale_factor),
        (in_blocks(query_low), in_blocks(key_all), in_blocks(value_all)),
    )
    attn_low = unblock(attn_out).reshape(row_count, width).astype(jnp.bfloat16)
    resid_mid = resid_in + jnp.dot(attn_low, w_out, preferred_element_type=jnp.float32) + bias_out
    ln_two_out, normed_two, inv_two = norm_forward(resid_mid, gain_two, bias_two)
    act_two = ln_two_out.astype(jnp.bfloat16)
    hidden_pre = jnp.dot(act_two, w_fc1, preferred_element_type=jnp.float32) + bias_fc1
    hidden_low = jax.nn.gelu(hidden_pre, approximate=False).astype(jnp.bfloat16)
    result = resid_mid + jnp.dot(hidden_low, w_fc2, preferred_element_type=jnp.float32) + bias_fc2
    out_tokens = result.astype(jnp.bfloat16).reshape(tokens.shape)
    regathered = lax.all_gather(shard_low, "group", axis=0, tiled=True)
    back_qkv, back_out, back_fc1, back_fc2 = split_params(regathered)[:4]
    grad_res = cotangent.astype(jnp.float32).reshape(row_count, width)
    grad_mlp = cotangent.reshape(row_count, width)
    d_bias_fc2 = jnp.sum(grad_res, 0)
    d_w_fc2 = cross_dot(hidden_low, grad_mlp)
    grad_pre = (back_dot(grad_mlp, back_fc2) * gelu_slope(hidden_pre)).astype(jnp.bfloat16)
    d_bias_fc1 = jnp.sum(grad_pre.astype(jnp.float32), 0)
    d_w_fc1 = cross_dot(act_two, grad_pre)
    grad_norm_two = back_dot(grad_pre, back_fc1)
    d_gain_two = jnp.sum(grad_norm_two * normed_two, 0)
    d_bias_two = jnp.sum(grad_norm_two, 0)
    grad_mid = grad_res + norm_backward(grad_norm_two, normed_two, inv_two, gain_two)
    grad_proj = grad_mid.astype(jnp.bfloat16)
    d_bias_out = jnp.sum(grad_proj.astype(jnp.float32), 0)
    d_w_out = cross_dot(attn_low, grad_proj)
    grad_attn = back_dot(grad_proj, back_out).astype(jnp.bfloat16).reshape(image_shape)
    grad_q, grad_k_all, grad_v_all = lax.map(
        partial(local_back, masks=head_masks, scale_factor=scale_factor),
        (
            in_blocks(query_low),
            in_blocks(key_all),
            in_blocks(value_all),
            in_blocks(grad_attn),
            log_sum,
        ),
    )
    grad_key, grad_value = (
        lax.psum_scatter(
            unblock(grad_k_all).astype(jnp.bfloat16), "group", scatter_dimension=1, tiled=True
        ).astype(jnp.float32),
        lax.psum_scatter(
            unblock(grad_v_all).astype(jnp.bfloat16), "group", scatter_dimension=1, tiled=True
        ).astype(jnp.float32),
    )
    grad_query_n = unblock(grad_q).reshape(head_shape).astype(jnp.bfloat16).astype(jnp.float32)
    grad_key_n = grad_key.reshape(head_shape).astype(jnp.bfloat16).astype(jnp.float32)
    grad_value_n = grad_value.reshape(row_count, width).astype(jnp.bfloat16).astype(jnp.float32)
    d_gain_query = jnp.sum(grad_query_n * query_normed, (0, 1))
    d_gain_key = jnp.sum(grad_key_n * key_normed, (0, 1))
    grad_query_pre = norm_backward(grad_query_n, query_normed, query_inv, gain_query).reshape(
        row_count, width
    )
    grad_key_pre = norm_backward(grad_key_n, key_normed, key_inv, gain_key).reshape(
        row_count, width
    )
    grad_qkv = jnp.concatenate([grad_query_pre, grad_key_pre, grad_value_n], 1).astype(jnp.bfloat16)
    d_bias_qkv = jnp.sum(grad_qkv.astype(jnp.float32), 0)
    d_w_qkv = cross_dot(act_one, grad_qkv)
    grad_norm_one = back_dot(grad_qkv, back_qkv)
    d_gain_one = jnp.sum(grad_norm_one * normed_one, 0)
    d_bias_one = jnp.sum(grad_norm_one, 0)
    grad_in = grad_mid + norm_backward(grad_norm_one, normed_one, inv_one, gain_one)
    grad_tokens = grad_in.astype(jnp.bfloat16).reshape(tokens.shape)
    local_grad = jnp.concatenate(
        [
            member.reshape(-1)
            for member in (
                d_w_qkv,
                d_w_out,
                d_w_fc1,
                d_w_fc2,
                d_gain_one,
                d_bias_one,
                d_bias_qkv,
                d_gain_query,
                d_gain_key,
                d_bias_out,
                d_gain_two,
                d_bias_two,
                d_bias_fc1,
                d_bias_fc2,
            )
        ]
    )
    group_grad = lax.psum_scatter(
        local_grad.astype(jnp.bfloat16), "group", scatter_dimension=0, tiled=True
    ).astype(jnp.float32)
    grad_total = lax.psum(group_grad, "replica")
    momentum_new = MOMENT * momentum + grad_total
    weight_new = weight - rate[0] * (grad_total + MOMENT * momentum_new)
    step_value = step[0].astype(jnp.float32)
    ema_decay = jnp.minimum(DECAY_MAX, (1.0 + step_value) / (10.0 + step_value))
    average_new = ema_decay * average + (1.0 - ema_decay) * weight_new
    return (
        out_tokens,
        grad_tokens,
        grad_total,
        momentum_new,
        average_new,
        weight_new,
        weight_new.astype(jnp.bfloat16),
    )


def solution(mesh):
    in_specs = (
        P("replica", "group", None),
        P("replica", "group", None),
        P("group"),
        P("group"),
        P("group"),
        P(),
        P(),
    )
    out_specs = (
        P("replica", "group", None),
        P("replica", "group", None),
        P("group"),
        P("group"),
        P("group"),
        P("group"),
        P("group"),
    )
    return jax.shard_map(
        per_device, mesh=mesh, in_specs=in_specs, out_specs=out_specs, check_vma=False
    )
```

profile of v0, /device:TPU:0, one launch (start us, length us, event | category | flops | bytes accessed | tf_op | source)
XLA Modules:
  0.0 935.1 jit_solution(8608521233848531671)
XLA Ops:
  8.8 10.9 %reshape.335 = bf16[1,1,443648]{2,1,0:T(2,128)(2,1)} reshape(bf16[443648]{0:T(1024)(128)(2,1)S(1)} %convert_element_type.177) | data formatting | bytes 1774592
  21.7 51.8 %all-gather.9.cloned.1.call-done = bf16[4,1,443648]{2,1,0:T(2,128)(2,1)} async-done(((bf16[1,1,443648]{2,1,0:T(2,128)(2,1)}), bf16[4,1,443648]{2,1,0:T(2,128)(2,1)}) %all-gather.9.cloned.1.call-update) | async-done | bytes 3549200 | tf_op jit(solution)/shard_map/all_gather | solution.py:183
  73.5 78.3 %reduce.13 = bf16[4,443648]{1,0:T(4,128)(2,1)} reduce(bf16[4,1,443648]{2,1,0:T(2,128)(2,1)} %all-gather.9.cloned.1.call-done, bf16[]{:T(256)} %constant.199), dimensions={1}, to_apply=%all-gather.reduce_sub_computation | reduce | bytes 7098370 | tf_op jit(solution)/shard_map/all_gather | solution.py:183
  151.8 3.3 reshape.336
  159.8 2.9 reshape.314
  163.9 2.0 convolution_add_fusion
  168.6 2.4 copy.69
  172.9 2.5 mul.382
  178.0 3.3 multiply_convert_fusion.1
  182.8 3.2 fusion.70
  186.3 3.2 reshape.322
  189.5 2.2 reshape.321
  196.5 2.9 multiply_convert_fusion.2
  201.5 3.7 copy.71
  205.2 17.9 %all-gather.7.cloned.1.call-done = bf16[2,1024,384]{2,1,0:T(8,128)(2,1)} async-done(((bf16[2,256,384]{2,1,0:T(8,128)(2,1)}), bf16[2,1024,384]{2,1,0:T(8,128)(2,1)}) %all-gather.7.cloned.1.call-update) | async-done | bytes 1572880 | tf_op jit(solution)/shard_map/all_gather | solution.py:233
  223.1 15.4 %while.48 = (s32[]{:T(128)}, f32[2,256,384]{2,1,0:T(8,128)S(1)}, f32[6,2,256]{2,1,0:T(2,128)S(1)}, bf16[6,384]{1,0:T(8,128)(2,1)S(1)}, bf16[2,256,384]{2,1,0:T(8...) while((s32[]{:T(128)}, f32[2,256,384]{2,1,0:T(8,128)S(1)}, ...), condition=%wide.region_9.10_spmd.clone, body=%wide.region_6.9_spmd.clone.sunk | while | flops 811400704 | bytes 17714324 | solution.py:102
  240.0 8.8 fusion.34
  248.8 2.3 fusion.73
  255.1 70.3 %while.49 = (s32[]{:T(128)}, f32[2,256,384]{2,1,0:T(8,128)}, f32[2,1024,384]{2,1,0:T(8,128)}, f32[2,1024,384]{2,1,0:T(8,128)}, bf16[6,384]{1,0:T(8,128)(2,1)S(1)...) while((s32[]{:T(128)}, f32[2,256,384]{2,1,0:T(8,128)}, ...), condition=%wide.region_16.17_spmd.clone, body=%wide.region_14.16_spmd.clone.sunk | while | flops 2023554560 | bytes 92814896 | solution.py:162
  255.3 2.1 fusion.125
  265.3 1.7 copy-done.4
  267.0 2.1 fusion.125
  278.7 2.1 fusion.125
  290.4 2.1 fusion.125
  302.1 2.1 fusion.125
  313.7 2.1 fusion.125
  325.4 2.1 convert_element_type.230
  327.5 61.8 %copy.90 = bf16[2,1024,384]{0,2,1:T(8,128)(2,1)} copy(bf16[2,1024,384]{2,1,0:T(8,128)(2,1)S(1)} %convert_element_type.230) | data formatting | bytes 3145728
  389.2 162.7 %reshape.337 = bf16[1024,768]{1,0:T(8,128)(2,1)} reshape(bf16[1024,384,2]{2,1,0:T(8,128)(2,1)} %bitcast.29) | data formatting | bytes 3145728
  557.2 2.4 copy.80
  565.1 2.5 convolution_convert_fusion
  570.6 3.5 convolution_convert_fusion.1
  574.1 3.7 reshape.329
  577.8 3.1 multiply_reduce_fusion.4
  586.1 56.0 %reshape.338 = bf16[256,384,2]{2,1,0:T(8,128)(2,1)} reshape(bf16[256,768]{1,0:T(8,128)(2,1)} %reduce-scatter.7.cloned.1.call-done) | data formatting | bytes 786432
  642.1 23.3 %copy.91 = bf16[2,256,384]{1,0,2:T(2,128)(2,1)S(1)} copy(bf16[2,256,384]{0,2,1:T(8,128)(2,1)} %bitcast.123) | data formatting | bytes 786432
  667.9 3.1 multiply_reduce_fusion.3
  674.7 2.3 copy.83
  678.0 2.3 copy.86
  680.4 4.6 fusion.57
  686.5 4.0 multiply_reduce_fusion.5
  692.1 2.8 reshape.327
  694.9 50.5 %concatenate.9 = bf16[1774592]{0:T(1024)(128)(2,1)} concatenate(bf16[442368]{0:T(1024)(128)(2,1)} %reshape.327, bf16[147456]{0:T(1024)(128)(2,1)} %reshape.328, bf16[589824]{0:T(1024)(128)(2,1)S(1)} %copy-done.38, bf16[589824]{0:T(1024)(128)(2,1)S(1)} %copy-done.37, bf16[384]{0:T(512)(128)(2,1)} %get-tuple-element.265, bf16[384]{0:T(512)(128)(2,1)} %get-tuple-element.274, ...), dimensions={0} | concatenate | bytes 7098368 | tf_op jit(solution)/shard_map/concatenate | solution.py:301
  747.3 73.6 %all-reduce.6.cloned.1.call-done = bf16[1774592]{0:T(1024)(128)(2,1)} async-done(((bf16[1774592]{0:T(1024)(128)(2,1)}), bf16[1774592]{0:T(1024)(128)(2,1)}) %all-reduce.6.cloned.1.call-update) | async-done | bytes 3549200
  820.9 2.9 dynamic-slice_convert_fusion
  825.2 3.2 fusion.49
  829.6 90.3 %all-reduce.4.cloned.1.call-done = f32[443648]{0:T(1024)} async-done(((f32[443648]{0:T(1024)}), f32[443648]{0:T(1024)}) %all-reduce.4.cloned.1.call-update) | async-done | bytes 1774608 | tf_op jit(solution)/shard_map/psum | solution.py:325
  919.8 4.0 fusion.69
  (420 shorter events, 136.3 us)
Async XLA Ops:
  7.2 66.3 %all-gather.9.cloned.1.call-start = ((), (), s32[]{:S(2)}) async-start(), calls=%async_computation.6 | async-start | bytes 8872960 | tf_op jit(solution)/shard_map/all_gather | solution.py:183
  8.8 11.0 %copy-start.15 = (bf16[2,256,384]{2,1,0:T(8,128)(2,1)S(1)}, bf16[2,256,384]{2,1,0:T(8,128)(2,1)}, u32[]{:S(2)}) copy-start(bf16[2,256,384]{2,1,0:T(8,128)(2,1)} %param.11) | copy-start | bytes 1179652
  19.7 181.8 %all-gather.5.cloned.1.call-start = ((), (), s32[]{:S(2)}) async-start(), calls=%async_computation.2 | async-start | bytes 1966080 | tf_op jit(solution)/shard_map/all_gather | solution.py:232
  155.1 8.7 copy-start.8
  159.8 18.2 %copy-start.60 = (f32[384]{0:T(512)}, f32[384]{0:T(512)S(1)}, u32[]{:S(2)}) copy-start(f32[384]{0:T(512)S(1)} %mul.385) | copy-start | bytes 4612
  165.9 16.0 %copy-start.6 = (f32[512,1152]{1,0:T(8,128)}, f32[512,1152]{1,0:T(8,128)S(1)}, u32[]{:S(2)}) copy-start(f32[512,1152]{1,0:T(8,128)S(1)} %convolution_add_fusion) | copy-start | bytes 7077892
  168.6 6.8 copy-start.9
  171.1 6.9 copy-start.54
  178.0 8.0 copy-start.32
  181.4 41.8 %all-gather.7.cloned.1.call-start = ((), (), s32[]{:S(2)}) async-start(), calls=%async_computation.3 | async-start | bytes 1966080 | tf_op jit(solution)/shard_map/all_gather | solution.py:233
  182.7 403.4 %reduce-scatter.7.cloned.1.call-start = ((), (), s32[]{:S(2)}) async-start(), calls=%async_computation.7 | async-start | bytes 1966080
  186.1 9.4 %copy-start.62 = (f32[384]{0:T(512)}, f32[384]{0:T(512)S(1)}, u32[]{:S(2)}) copy-start(f32[384]{0:T(512)S(1)} %mul.377) | copy-start | bytes 4612
  186.3 5.4 copy-start.29
  193.5 5.9 copy-start.26
  195.0 5.7 copy-start.27
  199.4 23.8 %copy-start.51 = (f32[2,256,384]{2,1,0:T(8,128)S(1)}, f32[2,256,384]{2,1,0:T(8,128)}, u32[]{:S(2)}) copy-start(f32[2,256,384]{2,1,0:T(8,128)} %custom-call) | copy-start | bytes 2359300
  223.1 15.6 %copy-start.16 = (bf16[2,256,384]{2,1,0:T(8,128)(2,1)S(1)}, bf16[2,256,384]{2,1,0:T(8,128)(2,1)}, u32[]{:S(2)}) copy-start(bf16[2,256,384]{2,1,0:T(8,128)(2,1)} %param.11) | copy-start | bytes 1179652
  223.1 15.6 %copy-start.67 = (f32[384]{0:T(512)S(1)}, f32[384]{0:T(512)}, u32[]{:S(2)}) copy-start(f32[384]{0:T(512)} %get-tuple-element.321) | copy-start | bytes 4612
  239.4 13.4 %copy-start.21 = (f32[512,384]{1,0:T(8,128)}, f32[512,384]{1,0:T(8,128)S(1)}, u32[]{:S(2)}) copy-start(f32[512,384]{1,0:T(8,128)S(1)} %get-tuple-element.338) | copy-start | bytes 2359300
  240.0 8.8 copy-start.45
  240.0 8.8 copy-start.46
  389.2 163.4 %copy-start.68 = (f32[1,2,2,128]{3,2,1,0:T(2,128)S(1)}, f32[1,2,2,128]{3,2,1,0:T(2,128)}, u32[]{:S(2)}) copy-start(f32[1,2,2,128]{3,2,1,0:T(2,128)} %get-tuple-element.335) | copy-start | bytes 6148
  389.2 164.0 %copy-start.69 = (f32[1,2,2,128]{3,2,1,0:T(2,128)S(1)}, f32[1,2,2,128]{3,2,1,0:T(2,128)}, u32[]{:S(2)}) copy-start(f32[1,2,2,128]{3,2,1,0:T(2,128)} %get-tuple-element.333) | copy-start | bytes 6148
  551.9 4.1 copy-start.28
  552.0 133.1 %reduce-scatter.5.cloned.1.call-start = ((), (), s32[]{:S(2)}) async-start(), calls=%async_computation.4 | async-start | bytes 1966080 | tf_op jit(solution)/shard_map/reduce_scatter | solution.py:278
  557.2 6.5 copy-start.2
  565.1 255.8 %all-reduce.6.cloned.1.call-start = ((), (), s32[]{:S(2)}) async-start(), calls=%async_computation.8 | async-start | bytes 7098368
  570.6 7.2 copy-start.34
  570.6 7.2 copy-start.35
  574.1 8.1 copy-start.12
  574.1 8.1 copy-start.57
  665.4 6.9 copy-start.10
  665.4 6.9 copy-start.55
  673.7 6.6 copy-start.7
  673.8 6.6 copy-start.61
  673.8 6.6 copy-start.63
  680.4 6.1 copy-start.17
  680.4 6.1 copy-start.65
  680.4 6.1 copy-start.66
  690.5 4.4 copy-start.37
  690.5 4.4 copy-start.38
  690.5 4.4 copy-start.75
  690.5 4.4 copy-start.76
  745.4 79.7 %copy-start.23 = (f32[512,384]{1,0:T(8,128)S(1)}, f32[512,384]{1,0:T(8,128)}, u32[]{:S(2)}) copy-start(f32[512,384]{1,0:T(8,128)} %copy-done.21) | copy-start | bytes 2359300
  745.4 79.7 %copy-start.47 = (bf16[1536,384]{1,0:T(8,128)(2,1)S(1)}, bf16[1536,384]{1,0:T(8,128)(2,1)}, u32[]{:S(2)}) copy-start(bf16[1536,384]{1,0:T(8,128)(2,1)} %reshape.322) | copy-start | bytes 3538948
  745.5 79.7 %copy-start.77 = (f32[384]{0:T(512)S(1)}, f32[384]{0:T(512)}, u32[]{:S(2)}) copy-start(f32[384]{0:T(512)} %get-tuple-element.318) | copy-start | bytes 4612
  745.5 174.4 %all-reduce.4.cloned.1.call-start = ((), (), s32[]{:S(2)}) async-start(), calls=%async_computation.5 | async-start | bytes 3555328 | tf_op jit(solution)/shard_map/psum | solution.py:325
  828.4 91.5 %copy-start.20 = (f32[443648]{0:T(1024)S(1)}, f32[443648]{0:T(1024)}, u32[]{:S(2)}) copy-start(f32[443648]{0:T(1024)} %param.13) | copy-start | bytes 5323780
  (78 other events, 153.7 us)
Sparse Core Ops, SparseCore 0:
  19.8 53.6 all-gather.8
  181.5 19.8 all-gather.4
  203.5 19.6 all-gather.6
  552.1 28.0 reduce-scatter.6
  583.1 28.0 reduce-scatter.4
  745.6 75.2 all-reduce.5
  825.1 94.7 all-reduce.3
where the time goes:
time: 944 us; the launch traced here: 935 us
  local copies, waits for them, and re-layouts  471 us (50%)
  waiting for transfers between devices  234 us (25%)
  other arithmetic  128 us (14%)
  matrix products  83.4 us (9%)
  between operations  17.3 us (2%)
    unnamed x164, local copies, waits for them, and re-layouts  332 us
    psum x1, waiting for transfers between devices, per_device(): grad_total = lax.psum(group_grad, 'replica')  90.3 us
    all_gather x1, other arithmetic, per_device(): gathered = lax.all_gather(shard_low, 'group', axis=0, tiled=True)  78.3 us
    unnamed x9, waiting for transfers between devices  73.7 us
    all_gather x1, waiting for transfers between devices, per_device(): gathered = lax.all_gather(shard_low, 'group', axis=0, tiled=True)  51.8 us
    concatenate x1, local copies, waits for them, and re-layouts, per_device(): jnp.concatenate([member.reshape(-1) for member in (d_w_qkv, d_w_out, d_w_...  50.5 us
    while x84, local copies, waits for them, and re-layouts  27.4 us
  transfers between devices with their start and end apart: 7, of which 4 were waited for; matrix products, arithmetic and copies ran while one was open for 17% of the time, Pallas kernels for 0%

commit v1 on v0

--- a/solution.py
+++ b/solution.py
@@ -13,6 +13,24 @@
 DECAY_MAX = 0.999
 INV_ROOT_TWO = 0.7071067811865476
 INV_ROOT_TAU = 0.3989422804014327
+
+
+def laid_out(parts, dim):
+    lengths = list(parts.shape[1:])
+    lengths[dim] *= parts.shape[0]
+    return jnp.moveaxis(parts, 0, dim).reshape(lengths)
+
+
+def grow_blocks(x, axis):
+    peers = lax.axis_size(axis)
+    parts = x[None]
+    for level in range(peers.bit_length() - 1):
+        apart = 1 << level
+        partner_block = lax.ppermute(parts, axis, [(i, i ^ apart) for i in range(peers)])
+        both = jnp.stack([parts, partner_block])
+        upper = lax.axis_index(axis) >> level & 1
+        parts = jnp.where(upper == 0, both, both[::-1]).reshape(-1, *x.shape)
+    return parts
 
 
 def split_params(flat_vec):
@@ -180,7 +198,7 @@
         return array.reshape((image_count,) + array.shape[2:])
 
     shard_low = weight.astype(jnp.bfloat16)
-    gathered = lax.all_gather(shard_low, "group", axis=0, tiled=True)
+    gathered = laid_out(grow_blocks(shard_low, "group"), 0)
     (
         w_qkv,
         w_out,

time: 944 us -> 1030 us (1.091)
  local copies, waits for them, and re-layouts: 471 us -> 511 us
  other arithmetic: 128 us -> 154 us
  waiting for transfers between devices: 234 us -> 247 us
    ppermute x0 -> x2, waiting for transfers between devices: none -> 37.9 us  [grow_blocks(): lax.ppermute(parts, axis, [(i, i ^ apart) for i in range(peers)])]
    all_gather x1, waiting for transfers between devices: 51.8 us -> 23.4 us  [per_device(): regathered = lax.all_gather(shard_low, 'group', axis=0, tiled=True)]
    another operation x0 -> x2, local copies, waits for them, and re-layouts: none -> 14.3 us  [the longest x1 10.1 us: grow_blocks(): both = jnp.stack([parts, partner_block])]
    another operation x2 -> x4, other arithmetic: 4.61 us -> 17.5 us  [the longest x2 12.9 us: grow_blocks(): both = jnp.stack([parts, partner_block])]
    broadcast_in_dim x0 -> x1, local copies, waits for them, and re-layouts: none -> 10.9 us  [grow_blocks(): parts = x[None]]
    select_n x0 -> x2, other arithmetic: none -> 10.4 us  [grow_blocks(): parts = jnp.where(upper == 0, both, both[::-1]).reshape(-1, *x.shape)]
    unnamed x164 -> x174, local copies, waits for them, and re-layouts: 332 us -> 328 us
  transfers between devices with their start and end apart: 7 -> 9, of which waited for: 4 -> 6; matrix products, arithmetic and copies ran while one was open for 17% -> 20% of each run, Pallas kernels for 0% -> 0%
where the time goes in v1:
time: 1030 us; the launch traced here: 1020 us
  local copies, waits for them, and re-layouts  511 us (50%)
  waiting for transfers between devices  247 us (24%)
  other arithmetic  154 us (15%)
  matrix products  85.8 us (8%)
  between operations  17.4 us (2%)
    unnamed x174, local copies, waits for them, and re-layouts  328 us
    psum x1, waiting for transfers between devices, per_device(): grad_total = lax.psum(group_grad, 'replica')  88.5 us
    all_gather x1, other arithmetic, per_device(): regathered = lax.all_gather(shard_low, 'group', axis=0, tiled=True)  78.3 us
    unnamed x9, waiting for transfers between devices  74.4 us
    concatenate x1, local copies, waits for them, and re-layouts, per_device(): jnp.concatenate([member.reshape(-1) for member in (d_w_qkv, d_w_out, d_w_...  50.4 us
    ppermute x2, waiting for transfers between devices, grow_blocks(): lax.ppermute(parts, axis, [(i, i ^ apart) for i in range(peers)])  37.9 us
    while x84, local copies, waits for them, and re-layouts  28.4 us
    all_gather x1, waiting for transfers between devices, per_device(): regathered = lax.all_gather(shard_low, 'group', axis=0, tiled=True)  23.4 us
  transfers between devices with their start and end apart: 9, of which 6 were waited for; matrix products, arithmetic and copies ran while one was open for 20% of the time, Pallas kernels for 0%

profile of v1, /device:TPU:0, one launch (start us, length us, event | category | flops | bytes accessed | tf_op | source)
XLA Modules:
  0.0 1019.1 jit_solution(11322637822011364521)
XLA Ops:
  8.8 10.9 %broadcast_in_dim.13 = bf16[1,443648]{1,0:T(2,128)(2,1)} reshape(bf16[443648]{0:T(1024)(128)(2,1)S(1)} %convert_element_type.177) | data formatting | bytes 1774592 | tf_op jit(solution)/shard_map/broadcast_in_dim | solution.py:26
  20.2 10.1 stack_broadcast_in_dim.3
  30.3 6.0 pad_maximum_fusion
  36.3 5.6 broadcast_select_fusion
  41.9 5.8 copy.124
  47.7 2.5 collective-permute-start.1
  51.8 37.9 %collective-permute-done.1 = bf16[2,443648]{1,0:T(2,128)(2,1)} collective-permute-done((bf16[2,443648]{1,0:T(2,128)(2,1)S(1)}, bf16[2,443648]{1,0:T(2,128)(2,1)}, u32[]{:S(2)}, u32[]{:S(2)}) %collective-permute-start.1) | collective-permute-done | bytes 1774624 | tf_op jit(solution)/shard_map/ppermute | solution.py:29
  89.7 6.9 pad_maximum_fusion.1
  96.6 4.8 broadcast_select_fusion.1
  101.4 4.2 reshape_reshape.2
  110.3 3.3 reshape.326
  119.6 2.5 copy.93
  123.9 2.5 mul.382
  129.0 3.3 multiply_convert_fusion.1
  135.4 2.9 fusion.71
  149.0 4.8 all-gather.5.cloned.1.call-done
  153.8 3.7 copy.95
  157.6 18.1 %all-gather.7.cloned.1.call-done = bf16[2,1024,384]{2,1,0:T(8,128)(2,1)} async-done(((bf16[2,256,384]{2,1,0:T(8,128)(2,1)}), bf16[2,1024,384]{2,1,0:T(8,128)(2,1)}) %all-gather.7.cloned.1.call-update) | async-done | bytes 1572880 | tf_op jit(solution)/shard_map/all_gather | solution.py:251
  175.6 19.3 %while.48 = (s32[]{:T(128)}, f32[2,256,384]{2,1,0:T(8,128)S(1)}, f32[6,2,256]{2,1,0:T(2,128)}, bf16[6,384]{1,0:T(8,128)(2,1)S(1)}, bf16[2,256,384]{2,1,0:T(8,128...) while((s32[]{:T(128)}, f32[2,256,384]{2,1,0:T(8,128)S(1)}, ...), condition=%wide.region_9.10_spmd.clone, body=%wide.region_6.9_spmd.clone.sunk | while | flops 811400704 | bytes 17714324 | solution.py:120
  196.3 9.0 fusion.34
  205.3 23.4 %all-gather.9.cloned.1.call-done = bf16[4,1,443648]{2,1,0:T(2,128)(2,1)} async-done(((bf16[1,1,443648]{2,1,0:T(2,128)(2,1)}), bf16[4,1,443648]{2,1,0:T(2,128)(2,1)}) %all-gather.9.cloned.1.call-update) | async-done | bytes 3549200 | tf_op jit(solution)/shard_map/all_gather | solution.py:265
  228.7 78.3 %reduce.13 = bf16[4,443648]{1,0:T(4,128)(2,1)} reduce(bf16[4,1,443648]{2,1,0:T(2,128)(2,1)} %all-gather.9.cloned.1.call-done, bf16[]{:T(256)} %constant.205), dimensions={1}, to_apply=%all-gather.reduce_sub_computation | reduce | bytes 7098370 | tf_op jit(solution)/shard_map/all_gather | solution.py:265
  307.0 5.1 reshape.352
  312.1 3.2 fusion.70
  316.2 3.5 reshape.339
  319.7 3.1 reshape.338
  322.8 4.3 fusion.74
  330.9 74.9 %while.49 = (s32[]{:T(128)}, f32[2,256,384]{2,1,0:T(8,128)}, f32[2,1024,384]{2,1,0:T(8,128)}, f32[2,1024,384]{2,1,0:T(8,128)}, bf16[6,384]{1,0:T(8,128)(2,1)S(1)...) while((s32[]{:T(128)}, f32[2,256,384]{2,1,0:T(8,128)}, ...), condition=%wide.region_16.17_spmd.clone, body=%wide.region_14.16_spmd.clone.sunk | while | flops 2023554560 | bytes 92814896 | solution.py:180
  407.9 61.9 %copy.114 = bf16[2,1024,384]{0,2,1:T(8,128)(2,1)} copy(bf16[2,1024,384]{2,1,0:T(8,128)(2,1)S(1)} %convert_element_type.230) | data formatting | bytes 3145728
  469.8 162.7 %reshape.353 = bf16[1024,768]{1,0:T(8,128)(2,1)} reshape(bf16[1024,384,2]{2,1,0:T(8,128)(2,1)} %bitcast.31) | data formatting | bytes 3145728
  635.5 2.4 copy.111
  640.2 2.3 copy.104
  644.0 2.4 convolution_convert_fusion
  654.7 3.4 convolution_convert_fusion.1
  658.1 3.7 reshape.345
  661.7 3.1 multiply_reduce_fusion.4
  670.1 56.0 %reshape.354 = bf16[256,384,2]{2,1,0:T(8,128)(2,1)} reshape(bf16[256,768]{1,0:T(8,128)(2,1)} %reduce-scatter.7.cloned.1.call-done) | data formatting | bytes 786432
  726.1 23.3 %copy.115 = bf16[2,256,384]{1,0,2:T(2,128)(2,1)S(1)} copy(bf16[2,256,384]{0,2,1:T(8,128)(2,1)} %bitcast.130) | data formatting | bytes 786432
  752.1 3.1 multiply_reduce_fusion.3
  764.5 4.6 fusion.57
  770.6 4.0 multiply_reduce_fusion.5
  776.3 2.8 reshape.343
  779.1 50.4 %concatenate.9 = bf16[1774592]{0:T(1024)(128)(2,1)} concatenate(bf16[442368]{0:T(1024)(128)(2,1)} %reshape.343, bf16[147456]{0:T(1024)(128)(2,1)} %reshape.344, bf16[589824]{0:T(1024)(128)(2,1)S(1)} %copy-done.38, bf16[589824]{0:T(1024)(128)(2,1)S(1)} %copy-done.37, bf16[384]{0:T(512)(128)(2,1)} %get-tuple-element.282, bf16[384]{0:T(512)(128)(2,1)} %get-tuple-element.291, ...), dimensions={0} | concatenate | bytes 7098368 | tf_op jit(solution)/shard_map/concatenate | solution.py:319
  831.4 73.6 %all-reduce.6.cloned.1.call-done = bf16[1774592]{0:T(1024)(128)(2,1)} async-done(((bf16[1774592]{0:T(1024)(128)(2,1)}), bf16[1774592]{0:T(1024)(128)(2,1)}) %all-reduce.6.cloned.1.call-update) | async-done | bytes 3549200
  905.0 2.9 dynamic-slice_convert_fusion
  910.7 3.5 fusion.49
  915.4 88.5 %all-reduce.4.cloned.1.call-done = f32[443648]{0:T(1024)} async-done(((f32[443648]{0:T(1024)}), f32[443648]{0:T(1024)}) %all-reduce.4.cloned.1.call-update) | async-done | bytes 1774608 | tf_op jit(solution)/shard_map/psum | solution.py:343
  1003.9 4.0 fusion.69
  (450 shorter events, 176.8 us)
Async XLA Ops:
  7.2 146.6 %all-gather.5.cloned.1.call-start = ((), (), s32[]{:S(2)}) async-start(), calls=%async_computation.2 | async-start | bytes 1966080 | tf_op jit(solution)/shard_map/all_gather | solution.py:250
  19.7 10.6 %collective-permute-start = (bf16[1,443648]{1,0:T(2,128)(2,1)}, bf16[1,443648]{1,0:T(2,128)(2,1)S(1)}, u32[]{:S(2)}, u32[]{:S(2)}) collective-permute-start(bf16[1,443648]{1,0:T(2,128)(2,1)} %broadcast_in_dim.13), channel_id=1, source_target_pairs={{0,8},{8,0},{16,24},{24,16},{1,9},{9,1},{17,25},{25,17},{2,10},{10... | collective-permute-start | bytes 2661896 | tf_op jit(solution)/shard_map/ppermute | solution.py:29
  30.3 6.0 copy-start.6
  41.9 8.3 copy-start.16
  47.7 42.0 %collective-permute-start.1 = (bf16[2,443648]{1,0:T(2,128)(2,1)S(1)}, bf16[2,443648]{1,0:T(2,128)(2,1)}, u32[]{:S(2)}, u32[]{:S(2)}) collective-permute-start(bf16[2,443648]{1,0:T(2,128)(2,1)S(1)} %bitcast.139), channel_id=1, source_target_pairs={{0,16},{8,24},{16,0},{24,8},{1,17},{9,25},{17,1},{25,9},{2,18},{10... | collective-permute-start | bytes 5323784 | tf_op jit(solution)/shard_map/ppermute | solution.py:29
  50.9 38.8 %copy-start.65 = (f32[2,256]{1,0:T(2,128)}, f32[2,256]{1,0:T(2,128)S(1)}, u32[]{:S(2)}) copy-start(f32[2,256]{1,0:T(2,128)S(1)} %get-tuple-element.357) | copy-start | bytes 6148
  105.7 9.1 copy-start.9
  110.3 18.7 %copy-start.61 = (f32[384]{0:T(512)}, f32[384]{0:T(512)S(1)}, u32[]{:S(2)}) copy-start(f32[384]{0:T(512)S(1)} %mul.385) | copy-start | bytes 4612
  116.8 15.6 %copy-start.7 = (f32[512,1152]{1,0:T(8,128)}, f32[512,1152]{1,0:T(8,128)S(1)}, u32[]{:S(2)}) copy-start(f32[512,1152]{1,0:T(8,128)S(1)} %convolution_add_fusion) | copy-start | bytes 7077892
  119.6 6.8 copy-start.10
  122.2 6.9 copy-start.55
  129.0 5.0 copy-start.31
  132.3 43.3 %all-gather.7.cloned.1.call-start = ((), (), s32[]{:S(2)}) async-start(), calls=%async_computation.3 | async-start | bytes 1966080 | tf_op jit(solution)/shard_map/all_gather | solution.py:251
  133.2 95.5 %all-gather.9.cloned.1.call-start = ((), (), s32[]{:S(2)}) async-start(), calls=%async_computation.6 | async-start | bytes 8872960 | tf_op jit(solution)/shard_map/all_gather | solution.py:265
  134.0 536.1 %reduce-scatter.7.cloned.1.call-start = ((), (), s32[]{:S(2)}) async-start(), calls=%async_computation.7 | async-start | bytes 1966080
  138.4 6.8 copy-start.63
  143.2 5.1 copy-start.26
  148.3 27.3 %copy-start.52 = (f32[2,256,384]{2,1,0:T(8,128)S(1)}, f32[2,256,384]{2,1,0:T(8,128)}, u32[]{:S(2)}) copy-start(f32[2,256,384]{2,1,0:T(8,128)} %custom-call) | copy-start | bytes 2359300
  175.6 19.3 %copy-start.17 = (bf16[2,256,384]{2,1,0:T(8,128)(2,1)S(1)}, bf16[2,256,384]{2,1,0:T(8,128)(2,1)}, u32[]{:S(2)}) copy-start(bf16[2,256,384]{2,1,0:T(8,128)(2,1)} %param.11) | copy-start | bytes 1179652
  175.6 19.4 %copy-start.45 = (bf16[384,384]{1,0:T(8,128)(2,1)S(1)}, bf16[384,384]{1,0:T(8,128)(2,1)}, u32[]{:S(2)}) copy-start(bf16[384,384]{1,0:T(8,128)(2,1)} %reshape.332) | copy-start | bytes 884740
  175.6 19.4 %copy-start.68 = (f32[384]{0:T(512)S(1)}, f32[384]{0:T(512)}, u32[]{:S(2)}) copy-start(f32[384]{0:T(512)} %get-tuple-element.340) | copy-start | bytes 4612
  195.7 133.0 %copy-start.22 = (f32[512,384]{1,0:T(8,128)}, f32[512,384]{1,0:T(8,128)S(1)}, u32[]{:S(2)}) copy-start(f32[512,384]{1,0:T(8,128)S(1)} %get-tuple-element.359) | copy-start | bytes 2359300
  195.9 132.7 %copy-start.75 = (f32[512]{0:T(512)}, f32[512]{0:T(512)S(1)}, u32[]{:S(2)}) copy-start(f32[512]{0:T(512)S(1)} %add_rsqrt_fusion.2) | copy-start | bytes 6148
  316.2 6.6 copy-start.44
  469.8 163.4 %copy-start.69 = (f32[1,2,2,128]{3,2,1,0:T(2,128)S(1)}, f32[1,2,2,128]{3,2,1,0:T(2,128)}, u32[]{:S(2)}) copy-start(f32[1,2,2,128]{3,2,1,0:T(2,128)} %get-tuple-element.356) | copy-start | bytes 6148
  469.8 164.0 %copy-start.70 = (f32[1,2,2,128]{3,2,1,0:T(2,128)S(1)}, f32[1,2,2,128]{3,2,1,0:T(2,128)}, u32[]{:S(2)}) copy-start(f32[1,2,2,128]{3,2,1,0:T(2,128)} %get-tuple-element.354) | copy-start | bytes 6148
  632.5 136.6 %reduce-scatter.5.cloned.1.call-start = ((), (), s32[]{:S(2)}) async-start(), calls=%async_computation.4 | async-start | bytes 1966080 | tf_op jit(solution)/shard_map/reduce_scatter | solution.py:296
  635.5 7.0 copy-start.2
  643.9 261.1 %all-reduce.6.cloned.1.call-start = ((), (), s32[]{:S(2)}) async-start(), calls=%async_computation.8 | async-start | bytes 7098368
  649.0 4.4 copy-start.15
  650.1 4.6 copy-start.23
  650.1 4.6 copy-start.76
  650.1 4.6 copy-start.83
  658.1 8.1 copy-start.13
  658.1 8.1 copy-start.58
  749.4 7.0 copy-start.11
  749.5 7.0 copy-start.56
  757.8 6.6 copy-start.8
  757.9 6.6 copy-start.62
  757.9 6.6 copy-start.64
  764.5 6.1 copy-start.18
  764.5 6.1 copy-start.66
  764.5 6.1 copy-start.67
  774.6 4.4 copy-start.37
  774.6 4.4 copy-start.38
  829.5 79.7 %copy-start.36 = (bf16[589824]{0:T(1024)(128)(2,1)S(1)}, bf16[589824]{0:T(1024)(128)(2,1)}, u32[]{:S(2)}) copy-start(bf16[589824]{0:T(1024)(128)(2,1)} %get-tuple-element.343) | copy-start | bytes 3538948
  829.5 174.4 %all-reduce.4.cloned.1.call-start = ((), (), s32[]{:S(2)}) async-start(), calls=%async_computation.5 | async-start | bytes 3555328 | tf_op jit(solution)/shard_map/psum | solution.py:343
  914.3 89.7 %copy-start.21 = (f32[443648]{0:T(1024)S(1)}, f32[443648]{0:T(1024)}, u32[]{:S(2)}) copy-start(f32[443648]{0:T(1024)} %param.13) | copy-start | bytes 5323780
  (87 other events, 191.3 us)
Sparse Core Ops, SparseCore 0:
  132.5 21.2 all-gather.4
  155.9 19.6 all-gather.6
  177.8 50.9 all-gather.8
  632.6 28.0 reduce-scatter.6
  663.7 27.9 reduce-scatter.4
  829.6 75.2 all-reduce.5
  909.2 94.7 all-reduce.3
